TPU v7x, 128 devices: a whole 4x4x4 slice. The times are simulated.
128 devices in a mesh: bucket: 8 (over y, core), member: 16 (over z, x).
Axes of the slice: x: 4, y: 4, z: 4, core: 2. Of those that a mesh axis runs over, the one named last changes fastest.
Arguments:
- loader_rows: float32 [8192, 4096], P(('bucket', 'member')), may hold values from -12 to 12
- dest_bucket: int32 [8192], P(('bucket', 'member')), may hold values from 0 to 7, as said below
- dest_slot: int32 [8192], P(('bucket', 'member')), may hold values from 0 to 127, as said below
- noise: float32 [32768, 4096], P(('bucket', 'member')), may hold values from -12 to 12
Outputs:
- targets: float32 [32768, 4096], P(('bucket', 'member'))
Inputs may be any that keep to these rules, and one draw needn't show every extreme that they name: Loaded row r goes to bucket group dest_bucket[r] on the device of that group with the same member index as its loader device. No loader device sends more than 16 rows to one bucket group; on every member index one bucket group receives exactly 16 rows from every loader device, and every bucket group is so filled on some member index. `dest_slot`: rows that reach the same device have distinct slots.
All inputs are finite; a program needn't handle non-finite values.
Results may differ from a plain program's by a relative error of at most 0.012.
The roundings to bfloat16 on the way count: a program that leaves them out, or rounds other values in their place, can miss the bound.
Values may be sent and summed in bfloat16 or wider, within the bound.
A program may use at most 128 MiB of HBM per device.

v0:
```python
import math
import jax
import jax.numpy as jnp
from jax import lax
from jax.sharding import PartitionSpec as P

ROWS_DEV = 128
ITERS = 4


def tile_cost(panel, noise_rows, noise_norm, width):
    cross_term = lax.dot_general(
        panel, noise_rows, (((1,), (1,)), ((), ())), preferred_element_type=jnp.float32
    )
    panel_wide = panel.astype(jnp.float32)
    return (
        jnp.sum(panel_wide * panel_wide, axis=1)[:, None] + noise_norm[None, :] - 2.0 * cross_term
    ) / width


def body(loader_rows, dest_bucket, dest_slot, noise):
    groups = lax.axis_size("bucket")
    width = loader_rows.shape[1]
    noise_count = noise.shape[0]
    capacity = ROWS_DEV // groups
    epsilon = 0.64 / math.sqrt(width)
    rounded = loader_rows.astype(jnp.bfloat16)
    hits = (dest_bucket[:, None] == jnp.arange(groups, dtype=jnp.int32)[None, :]).astype(jnp.int32)
    ranks = jnp.sum((jnp.cumsum(hits, axis=0) - 1) * hits, axis=1)
    position = dest_bucket * capacity + ranks
    send_rows = jnp.zeros((groups * capacity, width), jnp.bfloat16).at[position].set(rounded)
    send_slots = jnp.full((groups * capacity,), ROWS_DEV, jnp.int32).at[position].set(dest_slot)
    got_rows, got_slots = (
        lax.all_to_all(send_rows, "bucket", split_axis=0, concat_axis=0, tiled=True),
        lax.all_to_all(send_slots, "bucket", split_axis=0, concat_axis=0, tiled=True),
    )
    data_rows = jnp.zeros((ROWS_DEV, width), jnp.bfloat16).at[got_slots].set(got_rows, mode="drop")
    live_rows = (
        jnp.zeros((ROWS_DEV,), jnp.bfloat16)
        .at[got_slots]
        .set(jnp.ones(got_slots.shape, jnp.bfloat16), mode="drop")
    )
    noise_rows = noise.astype(jnp.bfloat16)
    noise_wide = noise_rows.astype(jnp.float32)
    noise_norm = jnp.sum(noise_wide * noise_wide, axis=1)
    whole_rows, whole_live = (
        lax.all_gather(data_rows, "member", axis=0, tiled=True),
        lax.all_gather(live_rows, "member", axis=0, tiled=True),
    )
    cost_tile = tile_cost(whole_rows, noise_rows, noise_norm, width)
    alive_rows = whole_live > 0.5
    col_pot = jnp.zeros((noise_count,), jnp.float32)
    exponent = jnp.zeros(cost_tile.shape, jnp.float32)
    col_total = jnp.ones((noise_count,), jnp.float32)
    for sweep_index in range(ITERS):
        scores = (col_pot[None, :] - cost_tile) / epsilon
        local_peak = jnp.max(scores, axis=1)
        row_peak = lax.pmax(local_peak, "member")
        row_total = lax.psum(jnp.sum(jnp.exp(scores - row_peak[:, None]), axis=1), "member")
        row_pot = -epsilon * (row_peak + jnp.log(row_total))
        col_scores = (row_pot[:, None] - cost_tile) / epsilon
        col_peak = jnp.max(jnp.where(alive_rows[:, None], col_scores, -jnp.inf), axis=0)
        exponent = jnp.where(alive_rows[:, None], jnp.exp(col_scores - col_peak[None, :]), 0.0)
        col_total = jnp.sum(exponent, axis=0)
        col_pot = -epsilon * (col_peak + jnp.log(col_total))
    weights = (exponent / col_total[None, :]).astype(jnp.bfloat16)
    targets = lax.dot_general(
        weights, whole_rows, (((0,), (0,)), ((), ())), preferred_element_type=jnp.float32
    )
    return targets


def solution(mesh):
    return jax.shard_map(
        body,
        mesh=mesh,
        in_specs=(
            P(("bucket", "member"), None),
            P(("bucket", "member")),
            P(("bucket", "member")),
            P(("bucket", "member"), None),
        ),
        out_specs=P(("bucket", "member"), None),
        check_vma=False,
    )
```

profile of v0, /device:TPU:2, one launch (start us, length us, event | category | flops | bytes accessed | tf_op | source)
XLA Modules:
  0.0 500.6 jit_solution(14216818540153028822)
XLA Ops:
  6.5 0.7 fusion.20
  7.4 0.8 select_reduce_fusion.7
  8.9 0.9 scatter_custom_fusion
  10.5 4.5 all-to-all-start
  14.9 3.1 scatter_custom_fusion.2
  18.0 2.2 all-to-all-done
  20.2 3.6 all-to-all-start.1
  25.2 14.4 %all-to-all-done.1 = bf16[8,16,4096]{2,1,0:T(8,128)(2,1)S(1)} async-done(((bf16[8,16,4096]{2,1,0:T(8,128)(2,1)}), bf16[8,16,4096]{2,1,0:T(8,128)(2,1)S(1)}, u32[]{:S(2)}, u32[]{:S(2)}) %all-to-all-start.1) | async-done | bytes 1048608 | tf_op jit(solution)/shard_map/all_to_all | solution.py:34
  39.6 3.0 scatter_custom_fusion.3
  42.7 2.6 multiply_reduce_fusion.1
  45.3 1.3 scatter_custom_fusion.1
  46.6 21.6 %all-gather = bf16[16,1,128]{2,1,0:T(2,128)(2,1)S(1)} all-gather(bf16[1,1,128]{2,1,0:T(2,128)(2,1)S(1)} %bitcast.16), channel_id=1, replica_groups=mesh['bucket'=8,'member'=16] {'member'}, dimensions={0}, use_global_device_ids=true | all-gather | bytes 4352 | tf_op jit(solution)/shard_map/all_gather | solution.py:48
  68.2 86.4 %all-gather.3.cloned.1.call-done = bf16[2048,4096]{1,0:T(8,128)(2,1)} async-done(((bf16[128,4096]{1,0:T(8,128)(2,1)}), bf16[2048,4096]{1,0:T(8,128)(2,1)}) %all-gather.3.cloned.1.call-update) | async-done | bytes 16777232 | tf_op jit(solution)/shard_map/all_gather | solution.py:47
  154.6 7.5 %multiply_reduce_fusion = f32[2048]{0:T(1024)S(1)} fusion(bf16[2048,4096]{1,0:T(8,128)(2,1)} %all-gather.3.cloned.1.call-done), kind=kLoop, calls=%fused_computation.4 | loop fusion | flops 25163776 | bytes 16785408 | tf_op jit(solution)/shard_map/reduce_sum | solution.py:17
  162.1 3.1 copy-done
  165.3 7.8 %fusion.2 = (f32[2048]{0:T(1024)S(1)}, f32[2048,256]{1,0:T(8,128)S(1)}) fusion(bf16[2048,4096]{1,0:T(8,128)(2,1)S(1)} %copy-done, f32[256,4096]{1,0:T(8,128)} %param.7, f32[256]{0:T(256)S(1)} %multiply_reduce_fusion.1, f32[2048]{0:T(1024)S(1)} %multiply_reduce_fusion), kind=kOutput, calls=%fused_computation.30 | convolution fusion | flops 4299683840 | bytes 23086080 | tf_op jit(solution)/shard_map/dot_general | solution.py:12
  173.1 36.8 %pmax.28 = f32[2048]{0:T(1024)S(1)} all-reduce(f32[2048]{0:T(1024)S(1)} %get-tuple-element.5), channel_id=1, replica_groups=mesh['bucket'=8,'member'=16] {'member'}, use_global_device_ids=true, to_apply=%region_9.10 | all-reduce | flops 2048 | bytes 16384 | tf_op jit(solution)/shard_map/pmax | solution.py:58
  209.9 0.8 exponential_reduce_fusion.3
  210.7 38.9 %psum.28 = f32[2048]{0:T(1024)S(1)} all-reduce(f32[2048]{0:T(1024)S(1)} %exponential_reduce_fusion.3), channel_id=1, replica_groups=mesh['bucket'=8,'member'=16] {'member'}, use_global_device_ids=true, to_apply=%region_11.12 | all-reduce | flops 2048 | bytes 16384 | tf_op jit(solution)/shard_map/psum | solution.py:59
  250.3 0.7 select_reduce_fusion.5
  251.4 36.0 %pmax.29 = f32[2048]{0:T(1024)S(1)} all-reduce(f32[2048]{0:T(1024)S(1)} %fusion.3), channel_id=1, replica_groups=mesh['bucket'=8,'member'=16] {'member'}, use_global_device_ids=true, to_apply=%region_15.16 | all-reduce | flops 2048 | bytes 16384 | tf_op jit(solution)/shard_map/pmax | solution.py:58
  287.4 0.8 exponential_reduce_fusion.2
  288.2 38.0 %psum.29 = f32[2048]{0:T(1024)S(1)} all-reduce(f32[2048]{0:T(1024)S(1)} %exponential_reduce_fusion.2), channel_id=1, replica_groups=mesh['bucket'=8,'member'=16] {'member'}, use_global_device_ids=true, to_apply=%region_17.18 | all-reduce | flops 2048 | bytes 16384 | tf_op jit(solution)/shard_map/psum | solution.py:59
  326.9 0.7 select_reduce_fusion.3
  328.0 36.0 %pmax.30 = f32[2048]{0:T(1024)S(1)} all-reduce(f32[2048]{0:T(1024)S(1)} %fusion.4), channel_id=1, replica_groups=mesh['bucket'=8,'member'=16] {'member'}, use_global_device_ids=true, to_apply=%region_21.22 | all-reduce | flops 2048 | bytes 16384 | tf_op jit(solution)/shard_map/pmax | solution.py:58
  364.0 0.8 exponential_reduce_fusion.1
  364.8 38.0 %psum.30 = f32[2048]{0:T(1024)S(1)} all-reduce(f32[2048]{0:T(1024)S(1)} %exponential_reduce_fusion.1), channel_id=1, replica_groups=mesh['bucket'=8,'member'=16] {'member'}, use_global_device_ids=true, to_apply=%region_23.24 | all-reduce | flops 2048 | bytes 16384 | tf_op jit(solution)/shard_map/psum | solution.py:59
  404.7 36.0 %pmax.31 = f32[2048]{0:T(1024)S(1)} all-reduce(f32[2048]{0:T(1024)S(1)} %fusion.5), channel_id=1, replica_groups=mesh['bucket'=8,'member'=16] {'member'}, use_global_device_ids=true, to_apply=%region_27.28 | all-reduce | flops 2048 | bytes 16384 | tf_op jit(solution)/shard_map/pmax | solution.py:58
  440.7 0.8 exponential_reduce_fusion
  441.5 38.2 %psum.31 = f32[2048]{0:T(1024)S(1)} all-reduce(f32[2048]{0:T(1024)S(1)} %exponential_reduce_fusion), channel_id=1, replica_groups=mesh['bucket'=8,'member'=16] {'member'}, use_global_device_ids=true, to_apply=%region_29.30 | all-reduce | flops 2048 | bytes 16384 | tf_op jit(solution)/shard_map/psum | solution.py:59
  480.5 0.7 fusion.6
  481.2 12.6 %fusion.7 = f32[256,4096]{1,0:T(8,128)} fusion(bf16[2048,4096]{1,0:T(8,128)(2,1)} %all-gather.3.cloned.1.call-done, f32[2048,256]{1,0:T(8,128)S(1)} %get-tuple-element.6, f32[256]{0:T(256)S(1)} %fusion.6, f32[256]{0:T(256)S(1)} %select_reduce_fusion, f32[2048]{0:T(1024)S(1)} %add_multiply_fusion, pred[2048]{0:T(1024)(128)(4,1)S(1)} %compare_bitcast_fusion), kind=kOutput, calls=%fused_computation.35 | convolution fusion | flops 4298113024 | bytes 23080960 | tf_op jit(solution)/shard_map/dot_general | solution.py:67
  (27 shorter events, 7.6 us)
Async XLA Ops:
  10.5 9.7 %all-to-all-start = ((s32[8,16,1]{1,2,0:T(1,128)}), s32[8,16,1]{1,2,0:T(1,128)S(1)}, u32[]{:S(2)}, u32[]{:S(2)}) async-start(s32[8,16,1]{1,2,0:T(1,128)} %bitcast), calls=%async_computation | async-start | bytes 8192 | tf_op jit(solution)/shard_map/all_to_all | solution.py:35
  20.2 19.5 %all-to-all-start.1 = ((bf16[8,16,4096]{2,1,0:T(8,128)(2,1)}), bf16[8,16,4096]{2,1,0:T(8,128)(2,1)S(1)}, u32[]{:S(2)}, u32[]{:S(2)}) async-start(bf16[8,16,4096]{2,1,0:T(8,128)(2,1)} %bitcast.4), calls=%async_computation.1 | async-start | bytes 2097152 | tf_op jit(solution)/shard_map/all_to_all | solution.py:34
  23.8 130.8 %all-gather.3.cloned.1.call-start = ((), (), s32[]{:S(2)}) async-start(), calls=%async_computation.2 | async-start | bytes 17825792 | tf_op jit(solution)/shard_map/all_gather | solution.py:47
  154.6 10.7 %copy-start = (bf16[2048,4096]{1,0:T(8,128)(2,1)S(1)}, bf16[2048,4096]{1,0:T(8,128)(2,1)}, u32[]{:S(2)}) copy-start(bf16[2048,4096]{1,0:T(8,128)(2,1)} %all-gather.3.cloned.1.call-done) | copy-start | bytes 50331652
Sparse Core Ops, SparseCore 0:
  42.8 111.7 all-gather.2
where the time goes:
time: 501 us
  blocking collectives  319 us (64%)
  waiting for transfers between devices  103 us (21%)
  other arithmetic  26.2 us (5%)
  matrix products  20.4 us (4%)
  between operations  13.7 us (3%)
  local copies, waits for them, and re-layouts  9.75 us (2%)
  starting transfers between devices  8.07 us (2%)
    psum x4, blocking collectives, body(): lax.psum(jnp.sum(jnp.exp(scores - row_peak[:, None]), axis=1), 'member')  153 us
    pmax x4, blocking collectives, body(): row_peak = lax.pmax(local_peak, 'member')  145 us
    all_gather x1, waiting for transfers between devices, body(): lax.all_gather(data_rows, 'member', axis=0, tiled=True)  86.4 us
    all_gather x1, blocking collectives, body(): lax.all_gather(live_rows, 'member', axis=0, tiled=True)  21.6 us
    all_to_all x1, waiting for transfers between devices, body(): lax.all_to_all(send_rows, 'bucket', split_axis=0, concat_axis=0, tiled=True)  14.4 us
    dot_general x1, matrix products, body(): lax.dot_general(weights, whole_rows, (((0,), (0,)), ((), ())), preferred_...  12.6 us
  transfers between devices with their start and end apart: 3, of which 3 were waited for; matrix products, arithmetic and copies ran while one was open for 2% of the time, Pallas kernels for 0%

commit v1 on v0

--- a/solution.py
+++ b/solution.py
@@ -56,7 +56,9 @@
         scores = (col_pot[None, :] - cost_tile) / epsilon
         local_peak = jnp.max(scores, axis=1)
         row_peak = lax.pmax(local_peak, "member")
-        row_total = lax.psum(jnp.sum(jnp.exp(scores - row_peak[:, None]), axis=1), "member")
+        row_total = jnp.sum(
+            lax.all_gather(jnp.sum(jnp.exp(scores - row_peak[:, None]), axis=1), "member"), axis=0
+        )
         row_pot = -epsilon * (row_peak + jnp.log(row_total))
         col_scores = (row_pot[:, None] - cost_tile) / epsilon
         col_peak = jnp.max(jnp.where(alive_rows[:, None], col_scores, -jnp.inf), axis=0)

time: 501 us -> 442 us (0.88)
  blocking collectives: 319 us -> 260 us
    psum x4 -> x0, blocking collectives: 153 us -> none  [body(): lax.psum(jnp.sum(jnp.exp(scores - row_peak[:, None]), axis=1), 'member')]
    all_gather x0 -> x4, blocking collectives: none -> 93.5 us  [body(): lax.all_gather(jnp.sum(jnp.exp(scores - row_peak[:, None]), axis=1), 'mem...]
where the time goes in v1:
time: 442 us; the launch traced here: 441 us
  blocking collectives  260 us (59%)
  waiting for transfers between devices  103 us (23%)
  other arithmetic  26.3 us (6%)
  matrix products  20.4 us (5%)
  between operations  13.7 us (3%)
  local copies, waits for them, and re-layouts  9.86 us (2%)
  starting transfers between devices  8.07 us (2%)
    pmax x4, blocking collectives, body(): row_peak = lax.pmax(local_peak, 'member')  145 us
    all_gather x4, blocking collectives, body(): lax.all_gather(jnp.sum(jnp.exp(scores - row_peak[:, None]), axis=1), 'mem...  93.5 us
    all_gather x1, waiting for transfers between devices, body(): lax.all_gather(data_rows, 'member', axis=0, tiled=True)  86.4 us
    all_gather x1, blocking collectives, body(): lax.all_gather(live_rows, 'member', axis=0, tiled=True)  21.6 us
    all_to_all x1, waiting for transfers between devices, body(): lax.all_to_all(send_rows, 'bucket', split_axis=0, concat_axis=0, tiled=True)  14.4 us
    dot_general x1, matrix products, body(): lax.dot_general(weights, whole_rows, (((0,), (0,)), ((), ())), preferred_...  12.6 us
  transfers between devices with their start and end apart: 3, of which 3 were waited for; matrix products, arithmetic and copies ran while one was open for 2% of the time, Pallas kernels for 0%

profile of v1, /device:TPU:2, one launch (start us, length us, event | category | flops | bytes accessed | tf_op | source)
XLA Modules:
  0.0 441.3 jit_solution(903284111159033024)
XLA Ops:
  6.5 0.7 fusion.20
  7.4 0.8 select_reduce_fusion.7
  8.9 0.9 scatter_custom_fusion
  10.5 4.5 %all-to-all-start = ((s32[8,16,1]{1,2,0:T(1,128)}), s32[8,16,1]{1,2,0:T(1,128)S(1)}, u32[]{:S(2)}, u32[]{:S(2)}) async-start(s32[8,16,1]{1,2,0:T(1,128)} %bitcast), calls=%async_computation | async-start | bytes 8192 | tf_op jit(solution)/shard_map/all_to_all | solution.py:35
  14.9 3.1 scatter_custom_fusion.2
  18.0 2.2 all-to-all-done
  20.2 3.6 all-to-all-start.1
  25.2 14.4 %all-to-all-done.1 = bf16[8,16,4096]{2,1,0:T(8,128)(2,1)S(1)} async-done(((bf16[8,16,4096]{2,1,0:T(8,128)(2,1)}), bf16[8,16,4096]{2,1,0:T(8,128)(2,1)S(1)}, u32[]{:S(2)}, u32[]{:S(2)}) %all-to-all-start.1) | async-done | bytes 1048608 | tf_op jit(solution)/shard_map/all_to_all | solution.py:34
  39.6 3.0 scatter_custom_fusion.3
  42.7 2.6 multiply_reduce_fusion.1
  45.3 1.3 scatter_custom_fusion.1
  46.6 21.6 %all-gather.4 = bf16[16,1,128]{2,1,0:T(2,128)(2,1)S(1)} all-gather(bf16[1,1,128]{2,1,0:T(2,128)(2,1)S(1)} %bitcast.16), channel_id=1, replica_groups=mesh['bucket'=8,'member'=16] {'member'}, dimensions={0}, use_global_device_ids=true | all-gather | bytes 4352 | tf_op jit(solution)/shard_map/all_gather | solution.py:48
  68.2 86.4 %all-gather.7.cloned.1.call-done = bf16[2048,4096]{1,0:T(8,128)(2,1)} async-done(((bf16[128,4096]{1,0:T(8,128)(2,1)}), bf16[2048,4096]{1,0:T(8,128)(2,1)}) %all-gather.7.cloned.1.call-update) | async-done | bytes 16777232 | tf_op jit(solution)/shard_map/all_gather | solution.py:47
  154.6 7.5 %multiply_reduce_fusion = f32[2048]{0:T(1024)S(1)} fusion(bf16[2048,4096]{1,0:T(8,128)(2,1)} %all-gather.7.cloned.1.call-done), kind=kLoop, calls=%fused_computation.4 | loop fusion | flops 25163776 | bytes 16785408 | tf_op jit(solution)/shard_map/reduce_sum | solution.py:17
  162.1 3.1 copy-done
  165.3 7.8 %fusion.2 = (f32[2048]{0:T(1024)S(1)}, f32[2048,256]{1,0:T(8,128)S(1)}) fusion(bf16[2048,4096]{1,0:T(8,128)(2,1)S(1)} %copy-done, f32[256,4096]{1,0:T(8,128)} %param.7, f32[256]{0:T(256)S(1)} %multiply_reduce_fusion.1, f32[2048]{0:T(1024)S(1)} %multiply_reduce_fusion), kind=kOutput, calls=%fused_computation.30 | convolution fusion | flops 4299683840 | bytes 23086080 | tf_op jit(solution)/shard_map/dot_general | solution.py:12
  173.1 36.8 %pmax.28 = f32[2048]{0:T(1024)S(1)} all-reduce(f32[2048]{0:T(1024)S(1)} %get-tuple-element.5), channel_id=1, replica_groups=mesh['bucket'=8,'member'=16] {'member'}, use_global_device_ids=true, to_apply=%region_9.10 | all-reduce | flops 2048 | bytes 16384 | tf_op jit(solution)/shard_map/pmax | solution.py:58
  209.9 0.8 exponential_reduce_fusion.3
  210.7 23.5 %all-gather = f32[32768]{0:T(1024)S(1)} all-gather(f32[2048]{0:T(1024)S(1)} %exponential_reduce_fusion.3), channel_id=2, replica_groups=mesh['bucket'=8,'member'=16] {'member'}, dimensions={0}, use_global_device_ids=true | all-gather | bytes 139264 | tf_op jit(solution)/shard_map/all_gather | solution.py:60
  235.0 0.7 select_reduce_fusion.5
  236.1 36.0 %pmax.29 = f32[2048]{0:T(1024)S(1)} all-reduce(f32[2048]{0:T(1024)S(1)} %fusion.3), channel_id=1, replica_groups=mesh['bucket'=8,'member'=16] {'member'}, use_global_device_ids=true, to_apply=%region_15.16 | all-reduce | flops 2048 | bytes 16384 | tf_op jit(solution)/shard_map/pmax | solution.py:58
  272.1 0.8 exponential_reduce_fusion.2
  272.9 23.3 %all-gather.1 = f32[32768]{0:T(1024)S(1)} all-gather(f32[2048]{0:T(1024)S(1)} %exponential_reduce_fusion.2), channel_id=3, replica_groups=mesh['bucket'=8,'member'=16] {'member'}, dimensions={0}, use_global_device_ids=true | all-gather | bytes 139264 | tf_op jit(solution)/shard_map/all_gather | solution.py:60
  297.0 0.7 select_reduce_fusion.3
  298.1 36.0 %pmax.30 = f32[2048]{0:T(1024)S(1)} all-reduce(f32[2048]{0:T(1024)S(1)} %fusion.4), channel_id=1, replica_groups=mesh['bucket'=8,'member'=16] {'member'}, use_global_device_ids=true, to_apply=%region_21.22 | all-reduce | flops 2048 | bytes 16384 | tf_op jit(solution)/shard_map/pmax | solution.py:58
  334.1 0.8 exponential_reduce_fusion.1
  334.9 23.3 %all-gather.2 = f32[32768]{0:T(1024)S(1)} all-gather(f32[2048]{0:T(1024)S(1)} %exponential_reduce_fusion.1), channel_id=4, replica_groups=mesh['bucket'=8,'member'=16] {'member'}, dimensions={0}, use_global_device_ids=true | all-gather | bytes 139264 | tf_op jit(solution)/shard_map/all_gather | solution.py:60
  360.0 36.0 %pmax.31 = f32[2048]{0:T(1024)S(1)} all-reduce(f32[2048]{0:T(1024)S(1)} %fusion.5), channel_id=1, replica_groups=mesh['bucket'=8,'member'=16] {'member'}, use_global_device_ids=true, to_apply=%region_27.28 | all-reduce | flops 2048 | bytes 16384 | tf_op jit(solution)/shard_map/pmax | solution.py:58
  396.0 0.8 exponential_reduce_fusion
  396.8 23.5 %all-gather.3 = f32[32768]{0:T(1024)S(1)} all-gather(f32[2048]{0:T(1024)S(1)} %exponential_reduce_fusion), channel_id=5, replica_groups=mesh['bucket'=8,'member'=16] {'member'}, dimensions={0}, use_global_device_ids=true | all-gather | bytes 139264 | tf_op jit(solution)/shard_map/all_gather | solution.py:60
  421.1 0.7 fusion.6
  421.8 12.6 %fusion.7 = f32[256,4096]{1,0:T(8,128)} fusion(bf16[2048,4096]{1,0:T(8,128)(2,1)} %all-gather.7.cloned.1.call-done, f32[2048,256]{1,0:T(8,128)S(1)} %get-tuple-element.6, f32[256]{0:T(256)S(1)} %fusion.6, f32[256]{0:T(256)S(1)} %select_reduce_fusion, f32[2048]{0:T(1024)S(1)} %add_multiply_fusion, pred[2048]{0:T(1024)(128)(4,1)S(1)} %compare_bitcast_fusion), kind=kOutput, calls=%fused_computation.35 | convolution fusion | flops 4298113024 | bytes 23080960 | tf_op jit(solution)/shard_map/dot_general | solution.py:69
  (35 shorter events, 7.8 us)
Async XLA Ops:
  10.5 9.7 %all-to-all-start = ((s32[8,16,1]{1,2,0:T(1,128)}), s32[8,16,1]{1,2,0:T(1,128)S(1)}, u32[]{:S(2)}, u32[]{:S(2)}) async-start(s32[8,16,1]{1,2,0:T(1,128)} %bitcast), calls=%async_computation | async-start | bytes 8192 | tf_op jit(solution)/shard_map/all_to_all | solution.py:35
  20.2 19.5 %all-to-all-start.1 = ((bf16[8,16,4096]{2,1,0:T(8,128)(2,1)}), bf16[8,16,4096]{2,1,0:T(8,128)(2,1)S(1)}, u32[]{:S(2)}, u32[]{:S(2)}) async-start(bf16[8,16,4096]{2,1,0:T(8,128)(2,1)} %bitcast.4), calls=%async_computation.1 | async-start | bytes 2097152 | tf_op jit(solution)/shard_map/all_to_all | solution.py:34
  23.8 130.8 %all-gather.7.cloned.1.call-start = ((), (), s32[]{:S(2)}) async-start(), calls=%async_computation.2 | async-start | bytes 17825792 | tf_op jit(solution)/shard_map/all_gather | solution.py:47
  154.6 10.7 %copy-start = (bf16[2048,4096]{1,0:T(8,128)(2,1)S(1)}, bf16[2048,4096]{1,0:T(8,128)(2,1)}, u32[]{:S(2)}) copy-start(bf16[2048,4096]{1,0:T(8,128)(2,1)} %all-gather.7.cloned.1.call-done) | copy-start | bytes 50331652
Sparse Core Ops, SparseCore 0:
  42.8 111.7 all-gather.6
